TPU v7x, 256 devices: a whole 4x4x8 slice. The times are simulated.
256 devices in a mesh: view: 32 (over z_lo, y, x), slab: 8 (over z_hi, core).
Axes of the slice: x: 4, y: 4, z: 8 (z_hi: 4, z_lo: 2; z = z_hi * 2 + z_lo), core: 2. Of those that a mesh axis runs over, the one named last changes fastest.
Arguments:
- tiles: bfloat16 [32, 8, 64, 128, 128], P('view', 'slab'), may hold values from 0 to 0.36621094
- tile_bin: int32 [32, 8, 64], P('view', 'slab'), may hold values from 0 to 7
- tile_vox: int32 [32, 8, 64], P('view', 'slab'), may hold values from 0 to 7
- tile_count: int32 [32, 8], P('view', 'slab'), may hold values from 8 to 64, as said below
- subset: int32 [256], P('view'), may hold values from 0 to 1, as said below
- pairs: int32 [2, 32768], P(None, 'view'), may hold values from 0 to 3359
- measured: float32 [32768, 128], P('view'), may hold values from 0.2 to 5
- background: float32 [32768], P('view'), may hold values from 0.3 to 3
- image: float32 [8192, 128], P('slab'), may hold values from 0.5 to 2
- efficiency: float32 [3360], P('view'), may hold values from 0.5 to 1.5
Outputs:
- image_out: float32 [8192, 128], P('slab')
- efficiency_out: float32 [3360], P('view')
Inputs may be any that keep to these rules, and one draw needn't show every extreme that they name: tiles at positions tile_count or later in a list are not part of the projector; some list is full in every draw. The 8 tile rows of bins of each view shard hold exactly 4 rows of each subset.
All inputs are finite; a program needn't handle non-finite values.
Results may differ from a plain program's by a relative error of at most 0.00079.
Values may be sent and summed in bfloat16 or wider, within the bound.
A program may use at most 64 MiB of HBM per device.

v0:
```python
import jax
import jax.numpy as jnp
from jax import lax
from jax.sharding import PartitionSpec as P

SUBSETS = 2


SMOOTH = 0.1
FAN_OFFSET = 1.0


def on_device(
    tiles, tile_bin, tile_vox, tile_count, subset, pairs, measured, background, image, efficiency
):
    blocks = tiles[0, 0]
    tile_num = blocks.shape[0]
    tile_edge = blocks.shape[1]
    frames = image.shape[1]
    vox_rows = image.shape[0]
    bin_rows = measured.shape[0]
    bin_blocks = bin_rows // tile_edge
    vox_blocks = vox_rows // tile_edge
    active = (jnp.arange(tile_num, dtype=jnp.int32) < tile_count[0, 0]).astype(jnp.float32)
    pick_bin = (tile_bin[0, 0][:, None] == jnp.arange(bin_blocks, dtype=jnp.int32)[None, :]).astype(
        jnp.float32
    ) * active[:, None]
    pick_vox = (tile_vox[0, 0][:, None] == jnp.arange(vox_blocks, dtype=jnp.int32)[None, :]).astype(
        jnp.float32
    ) * active[:, None]
    pick_vox_half = pick_vox.astype(jnp.bfloat16)
    highest = lax.Precision.HIGHEST

    def project(image_half, pick_out):
        picked = jnp.dot(
            pick_vox_half,
            image_half.reshape(vox_blocks, tile_edge * frames),
            preferred_element_type=jnp.float32,
        )
        picked = picked.astype(jnp.bfloat16).reshape(tile_num, tile_edge, frames)
        partial_value = jnp.einsum(
            "tij,tjf->tif", blocks, picked, preferred_element_type=jnp.float32
        )
        summed = jnp.dot(
            pick_out.T, partial_value.reshape(tile_num, tile_edge * frames), precision=highest
        )
        return summed.reshape(pick_out.shape[1] * tile_edge, frames)

    def forward_total(partial_value):
        return (lax.psum(partial_value, "slab"), 0)

    crystal_gain = lax.all_gather(efficiency, "view", axis=0, tiled=True)
    weight = crystal_gain[pairs[0]] * crystal_gain[pairs[1]]
    bin_subset = jnp.repeat(subset, tile_edge)
    estimate = image
    image_half = image.astype(jnp.bfloat16)
    for subset_index in range(SUBSETS):
        subset_weight = jnp.where(bin_subset == subset_index, weight, jnp.zeros_like(weight))
        summed, offset = forward_total(project(image_half, pick_bin))
        ratios = subset_weight[:, None] * measured
        ratios = ratios / (weight[:, None] * summed + background[:, None])
        ratios = ratios.astype(jnp.bfloat16)
        pick_half = pick_bin.astype(jnp.bfloat16)
        in_blocks = pick_bin.shape[1]
        backproject_picked = jnp.dot(
            pick_half,
            ratios.reshape(in_blocks, tile_edge * frames),
            preferred_element_type=jnp.float32,
        )
        backproject_picked = backproject_picked.astype(jnp.bfloat16).reshape(
            tile_num, tile_edge, frames
        )
        picked_weight = jnp.dot(
            pick_half,
            subset_weight.astype(jnp.bfloat16).reshape(in_blocks, tile_edge),
            preferred_element_type=jnp.float32,
        ).astype(jnp.bfloat16)
        image_part = jnp.einsum(
            "tij,tif->tjf", blocks, backproject_picked, preferred_element_type=jnp.float32
        )
        sens_part = jnp.einsum(
            "tij,ti->tj", blocks, picked_weight, preferred_element_type=jnp.float32
        )
        back_image = jnp.dot(
            pick_vox.T, image_part.reshape(tile_num, tile_edge * frames), precision=highest
        ).reshape(vox_rows, frames)
        sensitivity = jnp.dot(pick_vox.T, sens_part, precision=highest).reshape(vox_rows)
        back_image, sensitivity = (back_image, sensitivity)
        back_image, sensitivity = lax.psum((back_image, sensitivity), "view")
        estimate = estimate * (back_image + SMOOTH) / (sensitivity[:, None] + SMOOTH)
        image_half = estimate.astype(jnp.bfloat16)
    summed, offset = forward_total(project(image_half, pick_bin))
    expected = jnp.sum(weight[:, None] * summed + background[:, None], axis=1)
    counted = jnp.sum(measured, axis=1)
    crystals = crystal_gain.shape[0]
    fan_counts = jax.ops.segment_sum(
        counted, pairs[0], num_segments=crystals
    ) + jax.ops.segment_sum(counted, pairs[1], num_segments=crystals)
    fan_expected = jax.ops.segment_sum(
        expected, pairs[0], num_segments=crystals
    ) + jax.ops.segment_sum(expected, pairs[1], num_segments=crystals)
    fan_total = lax.psum_scatter(
        jnp.stack([fan_counts, fan_expected]), "view", scatter_dimension=1, tiled=True
    )
    updated = efficiency * (fan_total[0] + FAN_OFFSET) / (fan_total[1] + FAN_OFFSET)
    return (estimate, updated)


def solution(mesh):
    return jax.shard_map(
        on_device,
        mesh=mesh,
        in_specs=(
            P("view", "slab", None, None, None),
            P("view", "slab", None),
            P("view", "slab", None),
            P("view", "slab"),
            P("view"),
            P(None, "view"),
            P("view", None),
            P("view"),
            P("slab", None),
            P("view"),
        ),
        out_specs=(P("slab", None), P("view")),
        check_vma=False,
    )
```

profile of v0, /device:TPU:32, one launch (start us, length us, event | category | flops | bytes accessed | tf_op | source)
XLA Modules:
  0.0 1231.3 jit_solution(17105200055974249542)
XLA Ops:
  11.2 3.5 convolution_bitcast_fusion.4
  14.7 5.6 copy.28
  20.4 6.9 fusion.12
  30.0 157.1 %all-reduce = f32[3360]{0:T(1024)S(1)} all-reduce(f32[3360]{0:T(1024)S(1)} %dynamic-update-slice), channel_id=1, replica_groups=mesh['view'=32,'slab'=8] {'view'}, use_global_device_ids=true, to_apply=%add | all-reduce | flops 3360 | bytes 26880
  187.1 6.2 gather_fusion
  193.2 6.2 gather_fusion.1
  206.6 5.6 copy.30
  212.2 6.8 fusion.9
  221.2 78.1 %all-reduce.2 = (f32[1024]{0:T(1024)S(1)}, f32[1024]{0:T(1024)S(1)}) all-reduce(f32[1024]{0:T(1024)S(1)} %convolution_bitcast_fusion.6, f32[1024]{0:T(1024)S(1)} %convolution_bitcast_fusion.5), channel_id=1, replica_groups=mesh['view'=32,'slab'=8] {'view'}, use_global_device_ids=true, to_apply=%region_2.3 | all-reduce | flops 2048 | bytes 16384 | tf_op jit(solution)/shard_map/psum | solution.py:89
  299.3 232.5 %all-reduce.11.cloned.1.call-done = f32[1024,128]{1,0:T(8,128)} async-done(((f32[1024,128]{1,0:T(8,128)}), f32[1024,128]{1,0:T(8,128)}) %all-reduce.11.cloned.1.call-update) | async-done | bytes 524304 | tf_op jit(solution)/shard_map/psum | solution.py:89
  534.5 3.5 convolution_bitcast_fusion.2
  538.0 5.6 copy.32
  543.6 6.8 fusion.6
  551.4 74.7 %all-reduce.13.cloned.1.call-done = f32[1024,128]{1,0:T(8,128)} async-done(((f32[1024,128]{1,0:T(8,128)}), f32[1024,128]{1,0:T(8,128)}) %all-reduce.13.cloned.1.call-update) | async-done | bytes 524304 | tf_op jit(solution)/shard_map/psum | solution.py:50
  632.1 5.6 copy.34
  637.7 6.8 fusion.3
  646.4 311.6 %all-reduce.15.cloned.1.call-done = f32[1024,128]{1,0:T(8,128)} async-done(((f32[1024,128]{1,0:T(8,128)}), f32[1024,128]{1,0:T(8,128)}) %all-reduce.15.cloned.1.call-update) | async-done | bytes 524304 | tf_op jit(solution)/shard_map/psum | solution.py:89
  961.8 3.5 convolution_bitcast_fusion
  965.3 5.6 copy.36
  970.9 6.8 fusion
  978.7 11.2 scatter_custom_fusion
  990.0 63.5 %all-reduce.17.cloned.1.call-done = f32[1024,128]{1,0:T(8,128)} async-done(((f32[1024,128]{1,0:T(8,128)}), f32[1024,128]{1,0:T(8,128)}) %all-reduce.17.cloned.1.call-update) | async-done | bytes 524304 | tf_op jit(solution)/shard_map/psum | solution.py:50
  1055.0 11.2 scatter_custom_fusion.1
  1066.3 157.8 %all-reduce.1 = f32[2,3360]{1,0:T(2,128)S(1)} all-reduce(f32[2,3360]{1,0:T(2,128)S(1)} %pad_maximum_fusion), channel_id=2, replica_groups=mesh['view'=32,'slab'=8] {'view'}, use_global_device_ids=true, to_apply=%region_11.12.clone | all-reduce | flops 6720 | bytes 53760
  (86 shorter events, 32.0 us)
Async XLA Ops:
  7.2 4.0 copy-start
  7.2 193.4 %all-reduce.9.cloned.1.call-start = ((), (), s32[]{:S(2)}) async-start(), calls=%async_computation | async-start | bytes 1048576 | tf_op jit(solution)/shard_map/psum | solution.py:50
  14.7 5.6 copy-start.5
  20.4 7.9 copy-start.9
  20.4 7.9 copy-start.7
  20.4 9.3 copy-start.8
  20.4 166.6 %copy-start.4 = (s32[2,1024]{1,0:T(2,128)S(1)}, s32[2,1024]{1,0:T(2,128)}, u32[]{:S(2)}) copy-start(s32[2,1024]{1,0:T(2,128)} %param.15) | copy-start | bytes 24580
  28.2 503.6 %all-reduce.11.cloned.1.call-start = ((), (), s32[]{:S(2)}) async-start(), calls=%async_computation.1 | async-start | bytes 1048576 | tf_op jit(solution)/shard_map/psum | solution.py:89
  199.4 1.2 copy-start.2
  199.4 1.2 copy-start.3
  206.6 5.6 copy-start.6
  219.0 312.7 %copy-start.1 = (f32[1024,128]{1,0:T(8,128)S(1)}, f32[1024,128]{1,0:T(8,128)}, u32[]{:S(2)}) copy-start(f32[1024,128]{1,0:T(8,128)} %param.18) | copy-start | bytes 1572868
  219.9 406.2 %all-reduce.13.cloned.1.call-start = ((), (), s32[]{:S(2)}) async-start(), calls=%async_computation.2 | async-start | bytes 1048576 | tf_op jit(solution)/shard_map/psum | solution.py:50
  551.4 406.6 %all-reduce.15.cloned.1.call-start = ((), (), s32[]{:S(2)}) async-start(), calls=%async_computation.3 | async-start | bytes 1048576 | tf_op jit(solution)/shard_map/psum | solution.py:89
  645.4 408.1 %all-reduce.17.cloned.1.call-start = ((), (), s32[]{:S(2)}) async-start(), calls=%async_computation.4 | async-start | bytes 1048576 | tf_op jit(solution)/shard_map/psum | solution.py:50
Sparse Core Ops, SparseCore 0:
  28.3 75.9 all-reduce.8
  220.1 311.6 all-reduce.10
  551.5 74.6 all-reduce.12
  645.5 312.4 all-reduce.14
  978.8 74.6 all-reduce.16
where the time goes:
time: 1230 us
  waiting for transfers between devices  682 us (55%)
  blocking collectives  393 us (32%)
  matrix products  57.1 us (5%)
  local copies, waits for them, and re-layouts  49.3 us (4%)
  other arithmetic  32.8 us (3%)
  between operations  16.4 us (1%)
    psum x2, waiting for transfers between devices, on_device(): back_image, sensitivity = lax.psum((back_image, sensitivity), 'view')  544 us
    unnamed x2, blocking collectives  315 us
    psum x3, waiting for transfers between devices, forward_total(): return (lax.psum(partial_value, 'slab'), 0)  138 us
    psum x1, blocking collectives, on_device(): back_image, sensitivity = lax.psum((back_image, sensitivity), 'view')  78.1 us
  transfers between devices with their start and end apart: 5, of which 4 were waited for; matrix products, arithmetic and copies ran while one was open for 2% of the time, Pallas kernels for 0%

commit v1 on v0

v1 whole, which is shorter than its diff:
```python
import jax
import jax.numpy as jnp
from jax import lax
from jax.experimental import pallas as pl
from jax.experimental.pallas import tpu as pltpu
from jax.sharding import PartitionSpec as P

SUBSETS = 2
SMOOTH = 0.1
FAN_OFFSET = 1.0
MESH = pl.DeviceIdType.MESH
F32 = jnp.float32
BF16 = jnp.bfloat16
VMEM = pltpu.VMEM
SMEM = pltpu.SMEM

NV = 32
NS = 8
TB = 128
NB = 8
BINS = 1024
HALF = BINS // SUBSETS
VOX = 1024
FR = 128
FPART = FR // NS
VQ = 4
VW = VOX // VQ
OWN = 105

NN = (((1,), (0,)), ((), ()))
NT = (((1,), (1,)), ((), ()))
TN = (((0,), (0,)), ((), ()))


def dot(a, b, dims):
    return lax.dot_general(a, b, dims, preferred_element_type=F32)


def pieces(x):
    hi = x.astype(BF16)
    rest = x - hi.astype(F32)
    mid = rest.astype(BF16)
    low = (rest - mid.astype(F32)).astype(BF16)
    return hi, mid, low


def fan(values, oh_hi, oh_lo):
    parts = [jnp.where(oh_hi > 0, jnp.broadcast_to(p.astype(F32), oh_hi.shape), 0.0) for p in pieces(values)]
    lhs = jnp.concatenate(parts, axis=0).astype(BF16)
    out = dot(lhs, oh_lo, NT)
    return out[0:NV] + out[NV : 2 * NV] + out[2 * NV : 3 * NV]


def prepare(
    tile_bin, tile_vox, tile_count, subset, tiles, pairs, measured, background, image, efficiency,
    a_ref, part_ref, meas_ref, back_ref, hi_ref, lo_ref, est_ref, eff_ref, counts_ref,
    acc, img_t, meas_t, pair_s,
):
    v = lax.axis_index("view")
    s = lax.axis_index("slab")
    spots = []
    seen = [jnp.int32(0), jnp.int32(0)]
    for row in range(NB):
        k = subset[row]
        spots.append(jnp.where(k == 0, seen[0], NB // SUBSETS + seen[1]))
        seen = [seen[0] + jnp.where(k == 0, 1, 0), seen[1] + jnp.where(k == 0, 0, 1)]

    def spot_of(row):
        out = spots[0]
        for i in range(1, NB):
            out = jnp.where(row == i, spots[i], out)
        return out

    acc[...] = jnp.zeros_like(acc)

    @pl.loop(0, tile_count[0])
    def _(t):
        p = spot_of(tile_bin[t])
        cols = pl.ds(pl.multiple_of(tile_vox[t] * TB, TB), TB)
        acc[p, :, cols] += tiles[t].astype(F32)

    for row in range(NB):
        a_ref[pl.ds(row * TB, TB), :] = acc[row].astype(BF16)
        lanes = pl.ds(pl.multiple_of(spots[row] * TB, TB), TB)
        meas_t[:, lanes] = measured[pl.ds(row * TB, TB), :].T
        back_ref[:, lanes] = background[:, pl.ds(row * TB, TB)]
        pair_s[:, lanes] = pairs[:, pl.ds(row * TB, TB)]
        img_t[:, pl.ds(row * TB, TB)] = image[pl.ds(row * TB, TB), :].T

    meas_ref[...] = meas_t[pl.ds(pl.multiple_of(s * FPART, FPART), FPART), :]
    est_ref[...] = img_t[
        pl.ds(pl.multiple_of((v // VQ) * FPART, FPART), FPART),
        pl.ds(pl.multiple_of(lax.rem(v, VQ) * VW, VW), VW),
    ]
    eff_ref[...] = jnp.zeros_like(eff_ref)
    eff_ref[0, :, 0:OWN] = efficiency[...]

    ends = jnp.concatenate([pair_s[0:1, :], pair_s[1:2, :]], axis=1)
    high = jnp.floor((ends.astype(F32) + 0.5) * (1.0 / OWN)).astype(jnp.int32)
    low = ends - high * OWN
    oh_hi = jnp.where(lax.broadcasted_iota(jnp.int32, (NV, 2 * BINS), 0) == high, 1.0, 0.0)
    oh_lo = jnp.where(lax.broadcasted_iota(jnp.int32, (TB, 2 * BINS), 0) == low, 1.0, 0.0).astype(BF16)
    hi_ref[...] = oh_hi
    lo_ref[...] = oh_lo

    counted = jnp.sum(meas_t[...], axis=0, keepdims=True)
    counts_ref[...] = fan(jnp.concatenate([counted, counted], axis=1), oh_hi, oh_lo)

    part = dot(img_t[...].astype(BF16), a_ref[0:HALF, :], NT)
    part_ref[...] = part.astype(BF16).reshape(NS, FPART, HALF)


def exchange(
    a_ref, part_ref, meas_ref, back_ref, hi_ref, lo_ref, est_ref, eff_ref, counts_ref,
    out_ref, gain_ref,
    table, fwd_send, fwd, rat, sens_send, sens, bck_send, bck, img_send, img,
    sum_send, sums, fin_send, fin, q_send, q_recv, fan_send, fan_recv,
    send_sem, recv_sem,
):
    v = lax.axis_index("view")
    s = lax.axis_index("slab")
    barrier = pltpu.get_barrier_semaphore()

    def view_peer(i):
        return lax.rem(v + i, NV)

    def slab_peer(i):
        return lax.rem(s + i, NS)

    @pl.loop(1, NV)
    def _(i):
        pl.semaphore_signal(barrier, inc=1, device_id=(view_peer(i), s), device_id_type=MESH)

    @pl.loop(1, NS)
    def _(i):
        pl.semaphore_signal(barrier, inc=1, device_id=(v, slab_peer(i)), device_id_type=MESH)

    pl.semaphore_wait(barrier, NV - 1 + NS - 1)

    def to_views(phase, source, target):
        @pl.loop(1, NV)
        def _(i):
            w = view_peer(i)
            pltpu.make_async_remote_copy(
                src_ref=source(w), dst_ref=target, send_sem=send_sem.at[phase], recv_sem=recv_sem.at[phase],
                device_id=(w, s), device_id_type=MESH,
            ).start()

    def to_slabs(phase, source, target):
        @pl.loop(1, NS)
        def _(i):
            w = slab_peer(i)
            pltpu.make_async_remote_copy(
                src_ref=source(w), dst_ref=target, send_sem=send_sem.at[phase], recv_sem=recv_sem.at[phase],
                device_id=(v, w), device_id_type=MESH,
            ).start()

    def await_all(sem, ref):
        pltpu.make_async_copy(ref, ref, sem).wait()

    def views_of(ref):
        return ref.at[pl.ds(0, NV - 1)]

    def slabs_of(ref):
        return ref.at[pl.ds(0, NS - 1)]

    sent = [(0, slabs_of(fwd.at[0])), (1, views_of(table))]
    fi = v // VQ
    vi = lax.rem(v, VQ)
    frames = pl.ds(pl.multiple_of(fi * FPART, FPART), FPART)
    slot = vi * NS + fi

    to_slabs(0, lambda w: part_ref.at[w], fwd.at[0, s])
    to_views(1, lambda w: eff_ref.at[0], table.at[v])
    fwd[0, s] = part_ref[s]
    table[v] = eff_ref[0]

    await_all(recv_sem.at[1], views_of(table))
    rows = table[...].reshape(NV, TB)
    oh_hi = hi_ref[...]
    oh_lo = lo_ref[...]
    cols = jnp.concatenate([p.astype(F32) for p in pieces(rows)], axis=0).astype(BF16)
    hi3 = jnp.concatenate([oh_hi, oh_hi, oh_hi], axis=0).astype(BF16)
    picked = dot(cols, hi3, TN)
    ends = jnp.sum(jnp.where(oh_lo > 0, picked, 0.0), axis=0, keepdims=True)
    weight = ends[:, 0:BINS] * ends[:, BINS : 2 * BINS]
    back = back_ref[...]

    phase = 2
    for k in range(SUBSETS):
        bins = slice(k * HALF, (k + 1) * HALF)
        w_k = weight[:, bins]
        fwd_phase = 0 if k == 0 else phase
        if k > 0:
            total = jnp.zeros((FR, HALF), F32)
            for q in range(VQ):
                quarter = img[q * NS : (q + 1) * NS].reshape(FR, VW)
                total = total + dot(quarter, a_ref[bins, q * VW : (q + 1) * VW], NT)
            fwd_send[...] = total.astype(BF16).reshape(NS, FPART, HALF)
            to_slabs(phase, lambda w: fwd_send.at[w], fwd.at[k, s])
            fwd[k, s] = fwd_send[s]
            sent.append((phase, slabs_of(fwd.at[k])))
            phase += 1
        await_all(recv_sem.at[fwd_phase], slabs_of(fwd.at[k]))
        summed = jnp.sum(fwd[k].astype(F32), axis=0)
        ratio = (w_k * meas_ref[:, bins]) / (w_k * summed + back[:, bins])
        rat[k, s] = ratio.astype(BF16)
        to_slabs(phase, lambda w: rat.at[k, s], rat.at[k, s])
        rat_phase = phase
        sent.append((rat_phase, slabs_of(rat.at[k])))
        phase += 1

        if k == 0:
            row = lax.broadcasted_iota(jnp.int32, (16, BINS), 0)
            half = lax.broadcasted_iota(jnp.int32, (16, BINS), 1) // HALF
            lhs = jnp.where(row == half, jnp.broadcast_to(weight, (16, BINS)), 0.0).astype(BF16)
            both = dot(lhs, a_ref[...], NN)
            for q in range(VQ):
                sens_send[q] = both[0:SUBSETS, q * VW : (q + 1) * VW]
            sens_phase = phase
            phase += 1
            to_views(sens_phase, lambda w: sens_send.at[lax.rem(w, VQ)], sens.at[v])
            sens[v] = sens_send[vi]
            sent.append((sens_phase, views_of(sens)))

        await_all(recv_sem.at[rat_phase], slabs_of(rat.at[k]))
        lhs = rat[k].reshape(FR, HALF)
        for q in range(VQ):
            bck_send[k, q] = dot(lhs, a_ref[bins, q * VW : (q + 1) * VW], NN).astype(BF16)
        to_views(
            phase,
            lambda w: bck_send.at[k, lax.rem(w, VQ), pl.ds(pl.multiple_of((w // VQ) * FPART, FPART), FPART), :],
            bck.at[k, v],
        )
        bck[k, v] = bck_send[k, vi, frames, :]
        bck_phase = phase
        sent.append((bck_phase, views_of(bck.at[k])))
        phase += 1

        if k == 0:
            await_all(recv_sem.at[sens_phase], views_of(sens))
            sens_sum = jnp.sum(sens[...], axis=0)
            est = est_ref[...]
        await_all(recv_sem.at[bck_phase], views_of(bck.at[k]))
        back_image = jnp.sum(bck[k].astype(F32), axis=0)
        est = est * (back_image + SMOOTH) / (sens_sum[k : k + 1, :] + SMOOTH)
        half_image = est.astype(BF16)
        if k < SUBSETS - 1:
            img_send[...] = half_image
            to_views(phase, lambda w: img_send, img.at[slot])
            img[slot] = half_image
            await_all(recv_sem.at[phase], views_of(img))
            sent.append((phase, views_of(img)))
            phase += 1

    part_sum = jnp.sum(half_image.astype(F32), axis=0, keepdims=True)
    sum_send[...] = part_sum
    sum_phase = phase
    to_views(sum_phase, lambda w: sum_send, sums.at[v])
    sums[v] = part_sum
    fin_send[...] = est
    fin_phase = phase + 1
    to_views(fin_phase, lambda w: fin_send, fin.at[slot])
    fin[slot] = est
    sent += [(sum_phase, views_of(sums)), (fin_phase, views_of(fin))]
    phase += 2

    await_all(recv_sem.at[sum_phase], views_of(sums))
    quarter = []
    for q in range(VQ):
        total = sums[q]
        for f in range(1, NS):
            total = total + sums[f * VQ + q]
        quarter.append(total)
    image_sum = jnp.concatenate(quarter, axis=1)
    row = lax.broadcasted_iota(jnp.int32, (16, VOX), 0)
    hi, mid, low = [jnp.broadcast_to(p.astype(F32), (16, VOX)) for p in pieces(image_sum)]
    lhs = jnp.where(row == 0, hi, jnp.where(row == 1, mid, jnp.where(row == 2, low, 0.0))).astype(BF16)
    bins_sum = jnp.sum(dot(lhs, a_ref[...], NT), axis=0, keepdims=True)
    q_send[...] = bins_sum
    to_slabs(phase, lambda w: q_send, q_recv.at[s])
    q_recv[s] = bins_sum
    await_all(recv_sem.at[phase], slabs_of(q_recv))
    sent.append((phase, slabs_of(q_recv)))
    phase += 1
    final = jnp.sum(q_recv[...], axis=0)
    expected = weight * final + FR * back
    fan_exp = fan(jnp.concatenate([expected, expected], axis=1), oh_hi, oh_lo)
    fan_send[:, 0:1, :] = counts_ref[...].reshape(NV, 1, TB)
    fan_send[:, 1:2, :] = fan_exp.reshape(NV, 1, TB)
    to_views(phase, lambda w: fan_send.at[w], fan_recv.at[v])
    fan_recv[v] = fan_send[v]

    await_all(recv_sem.at[fin_phase], views_of(fin))
    for q in range(VQ):
        out_ref[pl.ds(q * VW, VW), :] = fin[q * NS : (q + 1) * NS].reshape(FR, VW).T

    await_all(recv_sem.at[phase], views_of(fan_recv))
    totals = jnp.sum(fan_recv[...], axis=0)
    gain = eff_ref[0] * (totals[0:1, :] + FAN_OFFSET) / (totals[1:2, :] + FAN_OFFSET)
    gain_ref[...] = gain[:, 0:OWN]
    sent.append((phase, views_of(fan_recv)))
    for number, ref in sent:
        await_all(send_sem.at[number], ref)


PHASES = 13


def on_device(
    tiles, tile_bin, tile_vox, tile_count, subset, pairs, measured, background, image, efficiency
):
    smem = pl.BlockSpec(memory_space=SMEM)
    vmem = pl.BlockSpec(memory_space=VMEM)
    shape = jax.ShapeDtypeStruct
    prepared = pl.pallas_call(
        prepare,
        out_shape=(
            shape((BINS, VOX), BF16),
            shape((NS, FPART, HALF), BF16),
            shape((FPART, BINS), F32),
            shape((1, BINS), F32),
            shape((NV, 2 * BINS), F32),
            shape((TB, 2 * BINS), BF16),
            shape((FPART, VW), F32),
            shape((1, 1, TB), F32),
            shape((NV, TB), F32),
        ),
        in_specs=[smem] * 4 + [vmem] * 6,
        out_specs=(vmem,) * 9,
        scratch_shapes=[
            VMEM((NB, TB, VOX), F32),
            VMEM((FR, VOX), F32),
            VMEM((FR, BINS), F32),
            VMEM((2, BINS), jnp.int32),
        ],
        name="prepare",
    )(
        tile_bin.reshape(-1),
        tile_vox.reshape(-1),
        tile_count.reshape(-1),
        subset,
        tiles.reshape(tiles.shape[2:]),
        pairs,
        measured,
        background.reshape(1, BINS),
        image,
        efficiency.reshape(1, OWN),
    )
    image_out, gain = pl.pallas_call(
        exchange,
        out_shape=(shape((VOX, FR), F32), shape((1, OWN), F32)),
        in_specs=[vmem] * 9,
        out_specs=(vmem, vmem),
        scratch_shapes=[
            VMEM((NV, 1, TB), F32),
            VMEM((NS, FPART, HALF), BF16),
            VMEM((SUBSETS, NS, FPART, HALF), BF16),
            VMEM((SUBSETS, NS, FPART, HALF), BF16),
            VMEM((VQ, SUBSETS, VW), F32),
            VMEM((NV, SUBSETS, VW), F32),
            VMEM((SUBSETS, VQ, FR, VW), BF16),
            VMEM((SUBSETS, NV, FPART, VW), BF16),
            VMEM((FPART, VW), BF16),
            VMEM((NV, FPART, VW), BF16),
            VMEM((1, VW), F32),
            VMEM((NV, 1, VW), F32),
            VMEM((FPART, VW), F32),
            VMEM((NV, FPART, VW), F32),
            VMEM((1, BINS), F32),
            VMEM((NS, 1, BINS), F32),
            VMEM((NV, 2, TB), F32),
            VMEM((NV, 2, TB), F32),
            pltpu.SemaphoreType.DMA((PHASES,)),
            pltpu.SemaphoreType.DMA((PHASES,)),
        ],
        compiler_params=pltpu.CompilerParams(collective_id=0, has_side_effects=True),
        name="exchange",
    )(*prepared)
    return image_out, gain.reshape(OWN)


def solution(mesh):
    return jax.shard_map(
        on_device,
        mesh=mesh,
        in_specs=(
            P("view", "slab", None, None, None),
            P("view", "slab", None),
            P("view", "slab", None),
            P("view", "slab"),
            P("view"),
            P(None, "view"),
            P("view", None),
            P("view"),
            P("slab", None),
            P("view"),
        ),
        out_specs=(P("slab", None), P("view")),
        check_vma=False,
    )
```

time: 1230 us -> 88 us (0.07)
  the two profiles are of different devices: /device:TPU:32 before, /device:TPU:1 now
where the time goes in v1:
time: 88 us; the launch traced here: 87.8 us
  Pallas kernels  83.5 us (95%)
  local copies, waits for them, and re-layouts  3.06 us (3%)
  between operations  1.29 us (1%)
    pallas_call x1, Pallas kernels, on_device(): pl.pallas_call(exchange, out_shape=(shape((VOX, FR), F32), shape((1, OWN)...  77.5 us
    pallas_call x1, Pallas kernels, on_device(): pl.pallas_call(prepare, out_shape=(shape((BINS, VOX), BF16), shape((NS, F...  5.96 us
    unnamed x2, local copies, waits for them, and re-layouts  3.06 us

profile of v1, /device:TPU:1, one launch (start us, length us, event | category | flops | bytes accessed | tf_op | source)
XLA Modules:
  0.0 87.8 jit_solution(17904993572420115742)
XLA Ops:
  1.3 6.0 %prepare.1 = (bf16[1024,1024]{1,0:T(8,128)(2,1)}, bf16[8,16,512]{2,1,0:T(8,128)(2,1)}, f32[16,1024]{1,0:T(8,128)}, f32[1,1024]{1,0:T(1,128)}, f32[32,2048]{1,0:T...) custom-call(s32[64]{0:T(128)} %bitcast.10, s32[64]{0:T(128)} %bitcast.11, ...), custom_call_target="tpu_custom_call" | custom-call | tf_op jit(solution)/shard_map/prepare/pallas_call | solution.py:316
  7.2 77.5 %exchange.1 = (f32[1024,128]{1,0:T(8,128)}, f32[1,105]{1,0:T(1,128)}) custom-call(bf16[1024,1024]{1,0:T(8,128)(2,1)} %get-tuple-element.13.a_ref, bf16[8,16,512]{2,1,0:T(8,128)(2,1)} %get-tuple-element.14.part_ref, f32[16,1024]{1,0:T(8,128)} %get-tuple-element.15.meas_ref, f32[1,1024]{1,0:T(1,128)} %get-tuple-element.16.back_ref, ...), custom_call_target="tpu_custom_call" | custom-call | tf_op jit(solution)/shard_map/exchange/pallas_call | solution.py:350
  84.8 1.9 %copy.15 = f32[1024,128]{1,0:T(8,128)} copy(f32[1024,128]{1,0:T(8,128)} %get-tuple-element.26) | data formatting | bytes 1048576
  86.6 1.2 %copy.16 = f32[105]{0:T(128)} copy(f32[105]{0:T(128)} %bitcast.13) | data formatting | bytes 840

commit v2 on v1

--- a/solution.py
+++ b/solution.py
@@ -51,13 +51,22 @@
     return out[0:NV] + out[NV : 2 * NV] + out[2 * NV : 3 * NV]
 
 
+CHUNKS = 4
+
+
 def prepare(
-    tile_bin, tile_vox, tile_count, subset, tiles, pairs, measured, background, image, efficiency,
-    a_ref, part_ref, meas_ref, back_ref, hi_ref, lo_ref, est_ref, eff_ref, counts_ref,
-    acc, img_t, meas_t, pair_s,
+    tile_bin, tile_vox, tile_count, subset, pairs, background, tiles,
+    a_ref, pair_ref, back_ref,
+    held, acc, half, in_sem, out_sem,
 ):
-    v = lax.axis_index("view")
-    s = lax.axis_index("slab")
+    size = held.shape[0] // CHUNKS
+
+    def fetch(c):
+        part = pl.ds(c * size, size)
+        return pltpu.make_async_copy(tiles.at[part], held.at[part], in_sem.at[c])
+
+    for c in range(CHUNKS):
+        fetch(c).start()
     spots = []
     seen = [jnp.int32(0), jnp.int32(0)]
     for row in range(NB):
@@ -71,54 +80,68 @@
             out = jnp.where(row == i, spots[i], out)
         return out
 
-    acc[...] = jnp.zeros_like(acc)
-
-    @pl.loop(0, tile_count[0])
-    def _(t):
-        p = spot_of(tile_bin[t])
-        cols = pl.ds(pl.multiple_of(tile_vox[t] * TB, TB), TB)
-        acc[p, :, cols] += tiles[t].astype(F32)
-
     for row in range(NB):
-        a_ref[pl.ds(row * TB, TB), :] = acc[row].astype(BF16)
+        acc[row] = jnp.zeros((TB, VOX), F32)
         lanes = pl.ds(pl.multiple_of(spots[row] * TB, TB), TB)
-        meas_t[:, lanes] = measured[pl.ds(row * TB, TB), :].T
         back_ref[:, lanes] = background[:, pl.ds(row * TB, TB)]
-        pair_s[:, lanes] = pairs[:, pl.ds(row * TB, TB)]
-        img_t[:, pl.ds(row * TB, TB)] = image[pl.ds(row * TB, TB), :].T
-
-    meas_ref[...] = meas_t[pl.ds(pl.multiple_of(s * FPART, FPART), FPART), :]
-    est_ref[...] = img_t[
-        pl.ds(pl.multiple_of((v // VQ) * FPART, FPART), FPART),
-        pl.ds(pl.multiple_of(lax.rem(v, VQ) * VW, VW), VW),
-    ]
-    eff_ref[...] = jnp.zeros_like(eff_ref)
-    eff_ref[0, :, 0:OWN] = efficiency[...]
-
-    ends = jnp.concatenate([pair_s[0:1, :], pair_s[1:2, :]], axis=1)
-    high = jnp.floor((ends.astype(F32) + 0.5) * (1.0 / OWN)).astype(jnp.int32)
-    low = ends - high * OWN
-    oh_hi = jnp.where(lax.broadcasted_iota(jnp.int32, (NV, 2 * BINS), 0) == high, 1.0, 0.0)
-    oh_lo = jnp.where(lax.broadcasted_iota(jnp.int32, (TB, 2 * BINS), 0) == low, 1.0, 0.0).astype(BF16)
-    hi_ref[...] = oh_hi
-    lo_ref[...] = oh_lo
-
-    counted = jnp.sum(meas_t[...], axis=0, keepdims=True)
-    counts_ref[...] = fan(jnp.concatenate([counted, counted], axis=1), oh_hi, oh_lo)
-
-    part = dot(img_t[...].astype(BF16), a_ref[0:HALF, :], NT)
-    part_ref[...] = part.astype(BF16).reshape(NS, FPART, HALF)
+        pair_ref[:, lanes] = pairs[:, pl.ds(row * TB, TB)]
+
+    for c in range(CHUNKS):
+        fetch(c).wait()
+
+        @pl.loop(c * size, jnp.minimum((c + 1) * size, tile_count[0, 0]))
+        def _(t):
+            p = spot_of(tile_bin[t])
+            cols = pl.ds(pl.multiple_of(tile_vox[t] * TB, TB), TB)
+            acc[p, :, cols] += held[t].astype(F32)
+
+    def put(row):
+        part = pl.ds(row * TB, TB)
+        return pltpu.make_async_copy(half.at[part], a_ref.at[part], out_sem.at[row])
+
+    for row in range(NB):
+        half[pl.ds(row * TB, TB), :] = acc[row].astype(BF16)
+        put(row).start()
+    for row in range(NB):
+        put(row).wait()
+
+
+def finish(image_ref, gain_ref, out_ref, gain_out, held, in_sem, out_sem):
+    size = VOX // CHUNKS
+
+    def move(c, inward):
+        part = pl.ds(c * size, size)
+        if inward:
+            return pltpu.make_async_copy(image_ref.at[part], held.at[part], in_sem.at[c])
+        return pltpu.make_async_copy(held.at[part], out_ref.at[part], out_sem.at[c])
+
+    for c in range(CHUNKS):
+        move(c, True).start()
+    gain_out[...] = gain_ref[...]
+    for c in range(CHUNKS):
+        move(c, True).wait()
+        move(c, False).start()
+    for c in range(CHUNKS):
+        move(c, False).wait()
 
 
 def exchange(
-    a_ref, part_ref, meas_ref, back_ref, hi_ref, lo_ref, est_ref, eff_ref, counts_ref,
-    out_ref, gain_ref,
+    subset, pair_ref, back_ref, efficiency, a_hbm, image_hbm, meas_hbm,
+    out_hbm, gain_ref,
+    a_ref, image, measured, img_t, meas_t, part_ref, eff_ref, out_ref,
     table, fwd_send, fwd, rat, sens_send, sens, bck_send, bck, img_send, img,
-    sum_send, sums, fin_send, fin, q_send, q_recv, fan_send, fan_recv,
-    send_sem, recv_sem,
+    sum_send, sums, fin, q_send, q_recv, fan_send, fan_recv,
+    send_sem, recv_sem, copy_sem,
 ):
     v = lax.axis_index("view")
     s = lax.axis_index("slab")
+    loads = [
+        pltpu.make_async_copy(image_hbm, image, copy_sem.at[0]),
+        pltpu.make_async_copy(a_hbm, a_ref, copy_sem.at[1]),
+        pltpu.make_async_copy(meas_hbm, measured, copy_sem.at[2]),
+    ]
+    for load in loads:
+        load.start()
     barrier = pltpu.get_barrier_semaphore()
 
     def view_peer(i):
@@ -135,6 +158,14 @@
     def _(i):
         pl.semaphore_signal(barrier, inc=1, device_id=(v, slab_peer(i)), device_id_type=MESH)
 
+    loads[0].wait()
+    for q in range(NB):
+        img_t[:, pl.ds(q * TB, TB)] = image[q].T
+    eff_ref[...] = jnp.zeros_like(eff_ref)
+    eff_ref[0, :, 0:OWN] = efficiency[...]
+    loads[1].wait()
+    first = dot(img_t[...].astype(BF16), a_ref[0:HALF, :], NT)
+    part_ref[...] = first.astype(BF16).reshape(NS, FPART, HALF)
     pl.semaphore_wait(barrier, NV - 1 + NS - 1)
 
     def to_views(phase, source, target):
@@ -165,8 +196,13 @@
         return ref.at[pl.ds(0, NS - 1)]
 
     sent = [(0, slabs_of(fwd.at[0])), (1, views_of(table))]
-    fi = v // VQ
+
+    def part_of(w):
+        return 2 * lax.rem(w // VQ, 4) + w // 16
+
+    z = v // 16
     vi = lax.rem(v, VQ)
+    fi = part_of(v)
     frames = pl.ds(pl.multiple_of(fi * FPART, FPART), FPART)
     slot = vi * NS + fi
 
@@ -175,10 +211,31 @@
     fwd[0, s] = part_ref[s]
     table[v] = eff_ref[0]
 
+    loads[2].wait()
+    spots = []
+    seen = [jnp.int32(0), jnp.int32(0)]
+    for row in range(NB):
+        k = subset[row]
+        spots.append(jnp.where(k == 0, seen[0], NB // SUBSETS + seen[1]))
+        seen = [seen[0] + jnp.where(k == 0, 1, 0), seen[1] + jnp.where(k == 0, 0, 1)]
+    for p in range(NB):
+        row = jnp.int32(0)
+        for r in range(1, NB):
+            row = jnp.where(spots[r] == p, r, row)
+        meas_t[:, pl.ds(p * TB, TB)] = measured[row].T
+    meas = meas_t[pl.ds(pl.multiple_of(s * FPART, FPART), FPART), :]
+    est0 = img_t[frames, pl.ds(pl.multiple_of(vi * VW, VW), VW)]
+    crystals = jnp.concatenate([pair_ref[0:1, :], pair_ref[1:2, :]], axis=1)
+    high = jnp.floor((crystals.astype(F32) + 0.5) * (1.0 / OWN)).astype(jnp.int32)
+    low = crystals - high * OWN
+    oh_hi = jnp.where(lax.broadcasted_iota(jnp.int32, (NV, 2 * BINS), 0) == high, 1.0, 0.0)
+    oh_lo = jnp.where(lax.broadcasted_iota(jnp.int32, (TB, 2 * BINS), 0) == low, 1.0, 0.0).astype(BF16)
+    counted = jnp.sum(meas_t[...], axis=0, keepdims=True)
+    counts = fan(jnp.concatenate([counted, counted], axis=1), oh_hi, oh_lo)
+    fan_send[:, 0:1, :] = counts.reshape(NV, 1, TB)
+
     await_all(recv_sem.at[1], views_of(table))
     rows = table[...].reshape(NV, TB)
-    oh_hi = hi_ref[...]
-    oh_lo = lo_ref[...]
     cols = jnp.concatenate([p.astype(F32) for p in pieces(rows)], axis=0).astype(BF16)
     hi3 = jnp.concatenate([oh_hi, oh_hi, oh_hi], axis=0).astype(BF16)
     picked = dot(cols, hi3, TN)
@@ -203,7 +260,7 @@
             phase += 1
         await_all(recv_sem.at[fwd_phase], slabs_of(fwd.at[k]))
         summed = jnp.sum(fwd[k].astype(F32), axis=0)
-        ratio = (w_k * meas_ref[:, bins]) / (w_k * summed + back[:, bins])
+        ratio = (w_k * meas[:, bins]) / (w_k * summed + back[:, bins])
         rat[k, s] = ratio.astype(BF16)
         to_slabs(phase, lambda w: rat.at[k, s], rat.at[k, s])
         rat_phase = phase
@@ -229,7 +286,7 @@
             bck_send[k, q] = dot(lhs, a_ref[bins, q * VW : (q + 1) * VW], NN).astype(BF16)
         to_views(
             phase,
-            lambda w: bck_send.at[k, lax.rem(w, VQ), pl.ds(pl.multiple_of((w // VQ) * FPART, FPART), FPART), :],
+            lambda w: bck_send.at[k, lax.rem(w, VQ), pl.ds(pl.multiple_of(part_of(w) * FPART, FPART), FPART), :],
             bck.at[k, v],
         )
         bck[k, v] = bck_send[k, vi, frames, :]
@@ -240,7 +297,7 @@
         if k == 0:
             await_all(recv_sem.at[sens_phase], views_of(sens))
             sens_sum = jnp.sum(sens[...], axis=0)
-            est = est_ref[...]
+            est = est0
         await_all(recv_sem.at[bck_phase], views_of(bck.at[k]))
         back_image = jnp.sum(bck[k].astype(F32), axis=0)
         est = est * (back_image + SMOOTH) / (sens_sum[k : k + 1, :] + SMOOTH)
@@ -258,14 +315,29 @@
     sum_phase = phase
     to_views(sum_phase, lambda w: sum_send, sums.at[v])
     sums[v] = part_sum
-    fin_send[...] = est
-    fin_phase = phase + 1
-    to_views(fin_phase, lambda w: fin_send, fin.at[slot])
-    fin[slot] = est
-    sent += [(sum_phase, views_of(sums)), (fin_phase, views_of(fin))]
-    phase += 2
-
+    pair_phase, fin_phase = phase + 1, phase + 2
+    phase += 3
+    partner = lax.rem(v + 16, NV)
+    fin[slot // 2, z] = est
+    pair_copy = pltpu.make_async_remote_copy(
+        src_ref=fin.at[slot // 2, z], dst_ref=fin.at[slot // 2, z],
+        send_sem=send_sem.at[pair_phase], recv_sem=recv_sem.at[pair_phase],
+        device_id=(partner, s), device_id_type=MESH,
+    )
+    pair_copy.start()
     await_all(recv_sem.at[sum_phase], views_of(sums))
+    sent.append((sum_phase, views_of(sums)))
+    pair_copy.wait_recv()
+
+    @pl.loop(1, 16)
+    def _(i):
+        w = 16 * z + lax.rem(lax.rem(v, 16) + i, 16)
+        pltpu.make_async_remote_copy(
+            src_ref=fin.at[slot // 2], dst_ref=fin.at[slot // 2],
+            send_sem=send_sem.at[fin_phase], recv_sem=recv_sem.at[fin_phase],
+            device_id=(w, s), device_id_type=MESH,
+        ).start()
+
     quarter = []
     for q in range(VQ):
         total = sums[q]
@@ -286,25 +358,32 @@
     final = jnp.sum(q_recv[...], axis=0)
     expected = weight * final + FR * back
     fan_exp = fan(jnp.concatenate([expected, expected], axis=1), oh_hi, oh_lo)
-    fan_send[:, 0:1, :] = counts_ref[...].reshape(NV, 1, TB)
     fan_send[:, 1:2, :] = fan_exp.reshape(NV, 1, TB)
     to_views(phase, lambda w: fan_send.at[w], fan_recv.at[v])
     fan_recv[v] = fan_send[v]
 
-    await_all(recv_sem.at[fin_phase], views_of(fin))
+    others = fin.at[pl.ds(0, 15)]
+    await_all(recv_sem.at[fin_phase], others)
     for q in range(VQ):
-        out_ref[pl.ds(q * VW, VW), :] = fin[q * NS : (q + 1) * NS].reshape(FR, VW).T
+        part = pl.ds(q * VW, VW)
+        out_ref[part, :] = fin[q * 4 : (q + 1) * 4].reshape(FR, VW).T
+        pltpu.make_async_copy(out_ref.at[part], out_hbm.at[part], copy_sem.at[3 + q]).start()
 
     await_all(recv_sem.at[phase], views_of(fan_recv))
     totals = jnp.sum(fan_recv[...], axis=0)
     gain = eff_ref[0] * (totals[0:1, :] + FAN_OFFSET) / (totals[1:2, :] + FAN_OFFSET)
     gain_ref[...] = gain[:, 0:OWN]
     sent.append((phase, views_of(fan_recv)))
+    sent.append((fin_phase, others))
     for number, ref in sent:
         await_all(send_sem.at[number], ref)
-
-
-PHASES = 13
+    pair_copy.wait_send()
+    for q in range(VQ):
+        part = pl.ds(q * VW, VW)
+        pltpu.make_async_copy(out_ref.at[part], out_hbm.at[part], copy_sem.at[3 + q]).wait()
+
+
+PHASES = 14
 
 
 def on_device(
@@ -312,47 +391,46 @@
 ):
     smem = pl.BlockSpec(memory_space=SMEM)
     vmem = pl.BlockSpec(memory_space=VMEM)
+    hbm = pl.BlockSpec(memory_space=pl.ANY)
     shape = jax.ShapeDtypeStruct
-    prepared = pl.pallas_call(
+    dma = pltpu.SemaphoreType.DMA
+    count = tiles.shape[2]
+    projector, ends, back = pl.pallas_call(
         prepare,
-        out_shape=(
-            shape((BINS, VOX), BF16),
-            shape((NS, FPART, HALF), BF16),
-            shape((FPART, BINS), F32),
-            shape((1, BINS), F32),
-            shape((NV, 2 * BINS), F32),
-            shape((TB, 2 * BINS), BF16),
-            shape((FPART, VW), F32),
-            shape((1, 1, TB), F32),
-            shape((NV, TB), F32),
-        ),
-        in_specs=[smem] * 4 + [vmem] * 6,
-        out_specs=(vmem,) * 9,
+        out_shape=(shape((BINS, VOX), BF16), shape((2, BINS), jnp.int32), shape((1, BINS), F32)),
+        in_specs=[smem] * 4 + [vmem, vmem, hbm],
+        out_specs=(hbm, vmem, vmem),
         scratch_shapes=[
+            VMEM((count, TB, TB), BF16),
             VMEM((NB, TB, VOX), F32),
-            VMEM((FR, VOX), F32),
-            VMEM((FR, BINS), F32),
-            VMEM((2, BINS), jnp.int32),
+            VMEM((BINS, VOX), BF16),
+            dma((CHUNKS,)),
+            dma((NB,)),
         ],
         name="prepare",
     )(
         tile_bin.reshape(-1),
         tile_vox.reshape(-1),
-        tile_count.reshape(-1),
+        tile_count,
         subset,
+        pairs,
+        background.reshape(1, BINS),
         tiles.reshape(tiles.shape[2:]),
-        pairs,
-        measured,
-        background.reshape(1, BINS),
-        image,
-        efficiency.reshape(1, OWN),
     )
     image_out, gain = pl.pallas_call(
         exchange,
         out_shape=(shape((VOX, FR), F32), shape((1, OWN), F32)),
-        in_specs=[vmem] * 9,
-        out_specs=(vmem, vmem),
+        in_specs=[smem, vmem, vmem, vmem, hbm, hbm, hbm],
+        out_specs=(hbm, vmem),
         scratch_shapes=[
+            VMEM((BINS, VOX), BF16),
+            VMEM((NB, TB, FR), F32),
+            VMEM((NB, TB, FR), F32),
+            VMEM((FR, VOX), F32),
+            VMEM((FR, BINS), F32),
+            VMEM((NS, FPART, HALF), BF16),
+            VMEM((1, 1, TB), F32),
+            VMEM((VOX, FR), F32),
             VMEM((NV, 1, TB), F32),
             VMEM((NS, FPART, HALF), BF16),
             VMEM((SUBSETS, NS, FPART, HALF), BF16),
@@ -365,18 +443,34 @@
             VMEM((NV, FPART, VW), BF16),
             VMEM((1, VW), F32),
             VMEM((NV, 1, VW), F32),
-            VMEM((FPART, VW), F32),
-            VMEM((NV, FPART, VW), F32),
+            VMEM((NV // 2, 2, FPART, VW), F32),
             VMEM((1, BINS), F32),
             VMEM((NS, 1, BINS), F32),
             VMEM((NV, 2, TB), F32),
             VMEM((NV, 2, TB), F32),
-            pltpu.SemaphoreType.DMA((PHASES,)),
-            pltpu.SemaphoreType.DMA((PHASES,)),
+            dma((PHASES,)),
+            dma((PHASES,)),
+            dma((3 + VQ,)),
         ],
         compiler_params=pltpu.CompilerParams(collective_id=0, has_side_effects=True),
         name="exchange",
-    )(*prepared)
+    )(
+        subset,
+        ends,
+        back,
+        efficiency.reshape(1, OWN),
+        projector,
+        image.reshape(NB, TB, FR),
+        measured.reshape(NB, TB, FR),
+    )
+    image_out, gain = pl.pallas_call(
+        finish,
+        out_shape=(shape((VOX, FR), F32), shape((1, OWN), F32)),
+        in_specs=[hbm, vmem],
+        out_specs=(hbm, vmem),
+        scratch_shapes=[VMEM((VOX, FR), F32), dma((CHUNKS,)), dma((CHUNKS,))],
+        name="finish",
+    )(image_out, gain)
     return image_out, gain.reshape(OWN)
 
 

time: 88 us -> 84.2 us (0.957)
  local copies, waits for them, and re-layouts: 3.06 us -> 0 us
    unnamed x2 -> x0, local copies, waits for them, and re-layouts: 3.06 us -> none
    pallas_call x1, Pallas kernels: 77.5 us -> 75.2 us  [on_device(): pl.pallas_call(exchange, out_shape=(shape((VOX, FR), F32), shape((1, OWN)...]
    pallas_call x1 -> x2, Pallas kernels: 5.96 us -> 7.47 us  [the longest x1 4.46 us: on_device(): pl.pallas_call(prepare, out_shape=(shape((BINS, VOX), BF16), shape((2, BI...]
where the time goes in v2:
time: 84.2 us; the launch traced here: 84 us
  Pallas kernels  82.7 us (98%)
  between operations  1.29 us (2%)
    pallas_call x1, Pallas kernels, on_device(): pl.pallas_call(exchange, out_shape=(shape((VOX, FR), F32), shape((1, OWN)...  75.2 us
    pallas_call x1, Pallas kernels, on_device(): pl.pallas_call(prepare, out_shape=(shape((BINS, VOX), BF16), shape((2, BI...  4.46 us
    pallas_call x1, Pallas kernels, on_device(): pl.pallas_call(finish, out_shape=(shape((VOX, FR), F32), shape((1, OWN),...  3 us

profile of v2, /device:TPU:1, one launch (start us, length us, event | category | flops | bytes accessed | tf_op | source)
XLA Modules:
  0.0 84.0 jit_solution(8555527331620906162)
XLA Ops:
  1.3 4.5 %prepare.1 = (bf16[1024,1024]{1,0:T(8,128)(2,1)}, s32[2,1024]{1,0:T(2,128)}, f32[1,1024]{1,0:T(1,128)}) custom-call(s32[64]{0:T(128)} %bitcast.12, s32[64]{0:T(128)} %bitcast.13, s32[1,1]{1,0:T(1,128)S(6)} %copy.12.tile_count, s32[8]{0:T(128)} %subset.3, s32[2,1024]{1,0:T(2,128)} %pairs.1, f32[1,1024]{1,0:T(1,128)} %bitcast.11, bf16[64,128,128]{2,1,0:T(8,128)(2,1)} %bitcast.8), custom_call_target="tpu_custom_call" | custom-call | tf_op jit(solution)/shard_map/prepare/pallas_call | solution.py:398
  5.7 75.2 %exchange.1 = (f32[1024,128]{1,0:T(8,128)}, f32[1,105]{1,0:T(1,128)}) custom-call(s32[8]{0:T(128)} %subset.3, s32[2,1024]{1,0:T(2,128)} %get-tuple-element.9.pair_ref, f32[1,1024]{1,0:T(1,128)} %get-tuple-element.10.back_ref, f32[1,105]{1,0:T(1,128)} %bitcast.14, bf16[1024,1024]{1,0:T(8,128)(2,1)} %get-tuple-element.11.a_hbm, f32[8,128,128]{2,1,0:T(8,128)} %bitcast.9, ...), custom_call_target="tpu_custom_call" | custom-call | tf_op jit(solution)/shard_map/exchange/pallas_call | solution.py:420
  81.0 3.0 %finish.1 = (f32[1024,128]{1,0:T(8,128)}, f32[1,105]{1,0:T(1,128)}) custom-call(f32[1024,128]{1,0:T(8,128)} %get-tuple-element.12.image_ref, f32[1,105]{1,0:T(1,128)} %get-tuple-element.13.gain_ref), custom_call_target="tpu_custom_call" | custom-call | tf_op jit(solution)/shard_map/finish/pallas_call | solution.py:466

commit v3 on v2

--- a/solution.py
+++ b/solution.py
@@ -51,84 +51,10 @@
     return out[0:NV] + out[NV : 2 * NV] + out[2 * NV : 3 * NV]
 
 
-CHUNKS = 4
-
-
-def prepare(
-    tile_bin, tile_vox, tile_count, subset, pairs, background, tiles,
-    a_ref, pair_ref, back_ref,
-    held, acc, half, in_sem, out_sem,
-):
-    size = held.shape[0] // CHUNKS
-
-    def fetch(c):
-        part = pl.ds(c * size, size)
-        return pltpu.make_async_copy(tiles.at[part], held.at[part], in_sem.at[c])
-
-    for c in range(CHUNKS):
-        fetch(c).start()
-    spots = []
-    seen = [jnp.int32(0), jnp.int32(0)]
-    for row in range(NB):
-        k = subset[row]
-        spots.append(jnp.where(k == 0, seen[0], NB // SUBSETS + seen[1]))
-        seen = [seen[0] + jnp.where(k == 0, 1, 0), seen[1] + jnp.where(k == 0, 0, 1)]
-
-    def spot_of(row):
-        out = spots[0]
-        for i in range(1, NB):
-            out = jnp.where(row == i, spots[i], out)
-        return out
-
-    for row in range(NB):
-        acc[row] = jnp.zeros((TB, VOX), F32)
-        lanes = pl.ds(pl.multiple_of(spots[row] * TB, TB), TB)
-        back_ref[:, lanes] = background[:, pl.ds(row * TB, TB)]
-        pair_ref[:, lanes] = pairs[:, pl.ds(row * TB, TB)]
-
-    for c in range(CHUNKS):
-        fetch(c).wait()
-
-        @pl.loop(c * size, jnp.minimum((c + 1) * size, tile_count[0, 0]))
-        def _(t):
-            p = spot_of(tile_bin[t])
-            cols = pl.ds(pl.multiple_of(tile_vox[t] * TB, TB), TB)
-            acc[p, :, cols] += held[t].astype(F32)
-
-    def put(row):
-        part = pl.ds(row * TB, TB)
-        return pltpu.make_async_copy(half.at[part], a_ref.at[part], out_sem.at[row])
-
-    for row in range(NB):
-        half[pl.ds(row * TB, TB), :] = acc[row].astype(BF16)
-        put(row).start()
-    for row in range(NB):
-        put(row).wait()
-
-
-def finish(image_ref, gain_ref, out_ref, gain_out, held, in_sem, out_sem):
-    size = VOX // CHUNKS
-
-    def move(c, inward):
-        part = pl.ds(c * size, size)
-        if inward:
-            return pltpu.make_async_copy(image_ref.at[part], held.at[part], in_sem.at[c])
-        return pltpu.make_async_copy(held.at[part], out_ref.at[part], out_sem.at[c])
-
-    for c in range(CHUNKS):
-        move(c, True).start()
-    gain_out[...] = gain_ref[...]
-    for c in range(CHUNKS):
-        move(c, True).wait()
-        move(c, False).start()
-    for c in range(CHUNKS):
-        move(c, False).wait()
-
-
 def exchange(
-    subset, pair_ref, back_ref, efficiency, a_hbm, image_hbm, meas_hbm,
-    out_hbm, gain_ref,
-    a_ref, image, measured, img_t, meas_t, part_ref, eff_ref, out_ref,
+    tile_count, subset, tile_bin, tile_vox, pairs, background, efficiency, tiles_hbm, image_hbm, meas_hbm,
+    out_ref, gain_ref,
+    a_ref, tiles, runs, keys, plan, plan_s, back_ref, pair_ref, image, measured, img_t, meas_t, part_ref, eff_ref,
     table, fwd_send, fwd, rat, sens_send, sens, bck_send, bck, img_send, img,
     sum_send, sums, fin, q_send, q_recv, fan_send, fan_recv,
     send_sem, recv_sem, copy_sem,
@@ -137,7 +63,7 @@
     s = lax.axis_index("slab")
     loads = [
         pltpu.make_async_copy(image_hbm, image, copy_sem.at[0]),
-        pltpu.make_async_copy(a_hbm, a_ref, copy_sem.at[1]),
+        pltpu.make_async_copy(tiles_hbm, tiles, copy_sem.at[1]),
         pltpu.make_async_copy(meas_hbm, measured, copy_sem.at[2]),
     ]
     for load in loads:
@@ -158,12 +84,66 @@
     def _(i):
         pl.semaphore_signal(barrier, inc=1, device_id=(v, slab_peer(i)), device_id_type=MESH)
 
+    spots = []
+    seen = [jnp.int32(0), jnp.int32(0)]
+    for row in range(NB):
+        k = subset[row]
+        spots.append(jnp.where(k == 0, seen[0], NB // SUBSETS + seen[1]))
+        seen = [seen[0] + jnp.where(k == 0, 1, 0), seen[1] + jnp.where(k == 0, 0, 1)]
+    rows_at = []
+    for p in range(NB):
+        row = jnp.int32(0)
+        for r in range(1, NB):
+            row = jnp.where(spots[r] == p, r, row)
+        rows_at.append(row)
+
+    count = tiles.shape[0]
+    where_bin = tile_bin[...]
+    key = jnp.zeros_like(where_bin)
+    for r in range(NB):
+        key = jnp.where(where_bin == r, spots[r], key)
+    key = key * NB + tile_vox[...]
+    live = lax.broadcasted_iota(jnp.int32, key.shape, 1) < tile_count[0, 0]
+    keys[...] = jnp.full_like(keys, NB * NB)
+    keys[:, 0:count] = jnp.where(live, key, NB * NB)
+    sub = lax.broadcasted_iota(jnp.int32, (TB, TB), 0)
+    lane = lax.broadcasted_iota(jnp.int32, (TB, TB), 1)
+    across = jnp.broadcast_to(keys[...], (TB, TB))
+    down = across.T
+    before = (down < across) | ((down == across) & (sub < lane))
+    rank = jnp.sum(jnp.where(before, 1, 0), axis=0, keepdims=True)
+    chosen = jnp.broadcast_to(rank, (TB, TB)).T == lane
+    plan[...] = jnp.zeros_like(plan)
+    plan[0:1, :] = jnp.sum(jnp.where(chosen, sub, 0), axis=0, keepdims=True)
+    plan[1:2, :] = jnp.sum(jnp.where(chosen, down, 0), axis=0, keepdims=True)
+    plan[2:3, :] = jnp.sum(jnp.where(down <= lane, 1, 0), axis=0, keepdims=True)
+    to_scalars = pltpu.make_async_copy(plan, plan_s, copy_sem.at[3])
+    to_scalars.start()
     loads[0].wait()
     for q in range(NB):
         img_t[:, pl.ds(q * TB, TB)] = image[q].T
     eff_ref[...] = jnp.zeros_like(eff_ref)
     eff_ref[0, :, 0:OWN] = efficiency[...]
+    to_scalars.wait()
     loads[1].wait()
+
+    def add_tile(r, total):
+        same = plan_s[1, r] == plan_s[1, jnp.maximum(r - 1, 0)]
+        total = total * jnp.where(same, 1.0, 0.0) + tiles[plan_s[0, r]].astype(F32)
+        runs[r] = total
+        return total
+
+    lax.fori_loop(0, count, add_tile, jnp.zeros((TB, TB), F32), unroll=2)
+
+    @pl.loop(0, NB * NB, unroll=2)
+    def _(d):
+        ends_at = plan_s[2, d]
+        starts_at = jnp.where(d == 0, 0, plan_s[2, jnp.maximum(d - 1, 0)])
+        kept = jnp.where(ends_at > starts_at, 1.0, 0.0)
+        block = runs[jnp.maximum(ends_at - 1, 0)] * kept
+        part = pl.ds(pl.multiple_of((d // NB) * TB, TB), TB)
+        a_ref[part, pl.ds(pl.multiple_of((d % NB) * TB, TB), TB)] = block.astype(BF16)
+
     first = dot(img_t[...].astype(BF16), a_ref[0:HALF, :], NT)
     part_ref[...] = first.astype(BF16).reshape(NS, FPART, HALF)
     pl.semaphore_wait(barrier, NV - 1 + NS - 1)
@@ -212,17 +192,16 @@
     table[v] = eff_ref[0]
 
     loads[2].wait()
-    spots = []
-    seen = [jnp.int32(0), jnp.int32(0)]
-    for row in range(NB):
-        k = subset[row]
-        spots.append(jnp.where(k == 0, seen[0], NB // SUBSETS + seen[1]))
-        seen = [seen[0] + jnp.where(k == 0, 1, 0), seen[1] + jnp.where(k == 0, 0, 1)]
     for p in range(NB):
-        row = jnp.int32(0)
+        part = pl.ds(p * TB, TB)
+        meas_t[:, part] = measured[rows_at[p]].T
+        noise = background[:, 0:TB]
+        pair = pairs[:, 0:TB]
         for r in range(1, NB):
-            row = jnp.where(spots[r] == p, r, row)
-        meas_t[:, pl.ds(p * TB, TB)] = measured[row].T
+            noise = jnp.where(spots[r] == p, background[:, r * TB : (r + 1) * TB], noise)
+            pair = jnp.where(spots[r] == p, pairs[:, r * TB : (r + 1) * TB], pair)
+        back_ref[:, part] = noise
+        pair_ref[:, part] = pair
     meas = meas_t[pl.ds(pl.multiple_of(s * FPART, FPART), FPART), :]
     est0 = img_t[frames, pl.ds(pl.multiple_of(vi * VW, VW), VW)]
     crystals = jnp.concatenate([pair_ref[0:1, :], pair_ref[1:2, :]], axis=1)
@@ -367,7 +346,6 @@
     for q in range(VQ):
         part = pl.ds(q * VW, VW)
         out_ref[part, :] = fin[q * 4 : (q + 1) * 4].reshape(FR, VW).T
-        pltpu.make_async_copy(out_ref.at[part], out_hbm.at[part], copy_sem.at[3 + q]).start()
 
     await_all(recv_sem.at[phase], views_of(fan_recv))
     totals = jnp.sum(fan_recv[...], axis=0)
@@ -378,9 +356,6 @@
     for number, ref in sent:
         await_all(send_sem.at[number], ref)
     pair_copy.wait_send()
-    for q in range(VQ):
-        part = pl.ds(q * VW, VW)
-        pltpu.make_async_copy(out_ref.at[part], out_hbm.at[part], copy_sem.at[3 + q]).wait()
 
 
 PHASES = 14
@@ -395,42 +370,26 @@
     shape = jax.ShapeDtypeStruct
     dma = pltpu.SemaphoreType.DMA
     count = tiles.shape[2]
-    projector, ends, back = pl.pallas_call(
-        prepare,
-        out_shape=(shape((BINS, VOX), BF16), shape((2, BINS), jnp.int32), shape((1, BINS), F32)),
-        in_specs=[smem] * 4 + [vmem, vmem, hbm],
-        out_specs=(hbm, vmem, vmem),
-        scratch_shapes=[
-            VMEM((count, TB, TB), BF16),
-            VMEM((NB, TB, VOX), F32),
-            VMEM((BINS, VOX), BF16),
-            dma((CHUNKS,)),
-            dma((NB,)),
-        ],
-        name="prepare",
-    )(
-        tile_bin.reshape(-1),
-        tile_vox.reshape(-1),
-        tile_count,
-        subset,
-        pairs,
-        background.reshape(1, BINS),
-        tiles.reshape(tiles.shape[2:]),
-    )
     image_out, gain = pl.pallas_call(
         exchange,
-        out_shape=(shape((VOX, FR), F32), shape((1, OWN), F32)),
-        in_specs=[smem, vmem, vmem, vmem, hbm, hbm, hbm],
-        out_specs=(hbm, vmem),
+        out_shape=(VMEM((VOX, FR), F32), VMEM((1, OWN), F32)),
+        in_specs=[smem, smem] + [vmem] * 5 + [hbm] * 3,
+        out_specs=(vmem, vmem),
         scratch_shapes=[
             VMEM((BINS, VOX), BF16),
+            VMEM((count, TB, TB), BF16),
+            VMEM((count, TB, TB), F32),
+            VMEM((1, TB), jnp.int32),
+            VMEM((8, TB), jnp.int32),
+            SMEM((8, TB), jnp.int32),
+            VMEM((1, BINS), F32),
+            VMEM((2, BINS), jnp.int32),
             VMEM((NB, TB, FR), F32),
             VMEM((NB, TB, FR), F32),
             VMEM((FR, VOX), F32),
             VMEM((FR, BINS), F32),
             VMEM((NS, FPART, HALF), BF16),
             VMEM((1, 1, TB), F32),
-            VMEM((VOX, FR), F32),
             VMEM((NV, 1, TB), F32),
             VMEM((NS, FPART, HALF), BF16),
             VMEM((SUBSETS, NS, FPART, HALF), BF16),
@@ -450,27 +409,22 @@
             VMEM((NV, 2, TB), F32),
             dma((PHASES,)),
             dma((PHASES,)),
-            dma((3 + VQ,)),
+            dma((4,)),
         ],
         compiler_params=pltpu.CompilerParams(collective_id=0, has_side_effects=True),
         name="exchange",
     )(
+        tile_count,
         subset,
-        ends,
-        back,
+        tile_bin.reshape(1, count),
+        tile_vox.reshape(1, count),
+        pairs,
+        background.reshape(1, BINS),
         efficiency.reshape(1, OWN),
-        projector,
+        tiles.reshape(tiles.shape[2:]),
         image.reshape(NB, TB, FR),
         measured.reshape(NB, TB, FR),
     )
-    image_out, gain = pl.pallas_call(
-        finish,
-        out_shape=(shape((VOX, FR), F32), shape((1, OWN), F32)),
-        in_specs=[hbm, vmem],
-        out_specs=(hbm, vmem),
-        scratch_shapes=[VMEM((VOX, FR), F32), dma((CHUNKS,)), dma((CHUNKS,))],
-        name="finish",
-    )(image_out, gain)
     return image_out, gain.reshape(OWN)
 
 

time: 84.2 us -> 76.1 us (0.904)
  Pallas kernels: 82.7 us -> 73.3 us
  local copies, waits for them, and re-layouts: 0 us -> 1.31 us
    pallas_call x3 -> x1, Pallas kernels: 82.7 us -> 73.3 us  [on_device(): pl.pallas_call(exchange, out_shape=(VMEM((VOX, FR), F32), VMEM((1, OWN),...]
    unnamed x0 -> x2, local copies, waits for them, and re-layouts: none -> 1.31 us
where the time goes in v3:
time: 76.1 us; the launch traced here: 75.9 us
  Pallas kernels  73.3 us (96%)
  local copies, waits for them, and re-layouts  1.31 us (2%)
  between operations  1.29 us (2%)
    pallas_call x1, Pallas kernels, on_device(): pl.pallas_call(exchange, out_shape=(VMEM((VOX, FR), F32), VMEM((1, OWN),...  73.3 us

profile of v3, /device:TPU:1, one launch (start us, length us, event | category | flops | bytes accessed | tf_op | source)
XLA Modules:
  0.0 75.9 jit_solution(4704140674585939159)
XLA Ops:
  1.3 73.3 %exchange.1 = (f32[1024,128]{1,0:T(8,128)S(1)}, f32[1,105]{1,0:T(1,128)S(1)}) custom-call(s32[1,1]{1,0:T(1,128)S(6)} %copy.16.tile_count, s32[8]{0:T(128)} %subset.1, s32[1,64]{1,0:T(1,128)} %bitcast.13, s32[1,64]{1,0:T(1,128)} %bitcast.14, s32[2,1024]{1,0:T(2,128)} %pairs.1, f32[1,1024]{1,0:T(1,128)} %bitcast.12, f32[1,105]{1,0:T(1,128)} %bitcast.15, ...), custom_call_target="tpu_custom_call" | custom-call | tf_op jit(solution)/shard_map/exchange/pallas_call | solution.py:373
  74.6 0.8 %copy.14 = f32[1024,128]{1,0:T(8,128)} copy(f32[1024,128]{1,0:T(8,128)S(1)} %get-tuple-element.6) | data formatting | bytes 1048576
  75.4 0.5 copy.15

commit v4 on v3

--- a/solution.py
+++ b/solution.py
@@ -22,7 +22,9 @@
 HALF = BINS // SUBSETS
 VOX = 1024
 FR = 128
-FPART = FR // NS
+STREAMS = 2
+FS = FR // STREAMS
+FPART = FS // NS
 VQ = 4
 VW = VOX // VQ
 OWN = 105
@@ -145,7 +147,7 @@
         a_ref[part, pl.ds(pl.multiple_of((d % NB) * TB, TB), TB)] = block.astype(BF16)
 
     first = dot(img_t[...].astype(BF16), a_ref[0:HALF, :], NT)
-    part_ref[...] = first.astype(BF16).reshape(NS, FPART, HALF)
+    part_ref[...] = first.reshape(STREAMS, NS, FPART, HALF).astype(BF16)
     pl.semaphore_wait(barrier, NV - 1 + NS - 1)
 
     def to_views(phase, source, target):
@@ -175,7 +177,17 @@
     def slabs_of(ref):
         return ref.at[pl.ds(0, NS - 1)]
 
-    sent = [(0, slabs_of(fwd.at[0])), (1, views_of(table))]
+    sent = []
+    numbers = iter(range(PHASES))
+
+    def new_phase(ref):
+        number = next(numbers)
+        sent.append((number, ref))
+        return number
+
+    def await_phase(number):
+        await_all(recv_sem.at[number], dict(sent)[number])
+
 
     def part_of(w):
         return 2 * lax.rem(w // VQ, 4) + w // 16
@@ -183,12 +195,16 @@
     z = v // 16
     vi = lax.rem(v, VQ)
     fi = part_of(v)
-    frames = pl.ds(pl.multiple_of(fi * FPART, FPART), FPART)
     slot = vi * NS + fi
 
-    to_slabs(0, lambda w: part_ref.at[w], fwd.at[0, s])
-    to_views(1, lambda w: eff_ref.at[0], table.at[v])
-    fwd[0, s] = part_ref[s]
+    fwd_at = [new_phase(slabs_of(fwd.at[0, h])) for h in range(STREAMS)]
+    eff_at = new_phase(views_of(table))
+    to_slabs(fwd_at[0], lambda w: part_ref.at[0, w], fwd.at[0, 0, s])
+    to_views(eff_at, lambda w: eff_ref.at[0], table.at[v])
+    for h in range(1, STREAMS):
+        to_slabs(fwd_at[h], lambda w: part_ref.at[h, w], fwd.at[0, h, s])
+    for h in range(STREAMS):
+        fwd[0, h, s] = part_ref[h, s]
     table[v] = eff_ref[0]
 
     loads[2].wait()
@@ -202,8 +218,9 @@
             pair = jnp.where(spots[r] == p, pairs[:, r * TB : (r + 1) * TB], pair)
         back_ref[:, part] = noise
         pair_ref[:, part] = pair
-    meas = meas_t[pl.ds(pl.multiple_of(s * FPART, FPART), FPART), :]
-    est0 = img_t[frames, pl.ds(pl.multiple_of(vi * VW, VW), VW)]
+    meas = [meas_t[pl.ds(pl.multiple_of(h * FS + s * FPART, FPART), FPART), :] for h in range(STREAMS)]
+    own = pl.ds(pl.multiple_of(vi * VW, VW), VW)
+    est = [img_t[pl.ds(pl.multiple_of(h * FS + fi * FPART, FPART), FPART), own] for h in range(STREAMS)]
     crystals = jnp.concatenate([pair_ref[0:1, :], pair_ref[1:2, :]], axis=1)
     high = jnp.floor((crystals.astype(F32) + 0.5) * (1.0 / OWN)).astype(jnp.int32)
     low = crystals - high * OWN
@@ -213,7 +230,7 @@
     counts = fan(jnp.concatenate([counted, counted], axis=1), oh_hi, oh_lo)
     fan_send[:, 0:1, :] = counts.reshape(NV, 1, TB)
 
-    await_all(recv_sem.at[1], views_of(table))
+    await_phase(eff_at)
     rows = table[...].reshape(NV, TB)
     cols = jnp.concatenate([p.astype(F32) for p in pieces(rows)], axis=0).astype(BF16)
     hi3 = jnp.concatenate([oh_hi, oh_hi, oh_hi], axis=0).astype(BF16)
@@ -222,29 +239,29 @@
     weight = ends[:, 0:BINS] * ends[:, BINS : 2 * BINS]
     back = back_ref[...]
 
-    phase = 2
     for k in range(SUBSETS):
         bins = slice(k * HALF, (k + 1) * HALF)
         w_k = weight[:, bins]
-        fwd_phase = 0 if k == 0 else phase
+        rat_at, bck_at = [], []
         if k > 0:
-            total = jnp.zeros((FR, HALF), F32)
-            for q in range(VQ):
-                quarter = img[q * NS : (q + 1) * NS].reshape(FR, VW)
-                total = total + dot(quarter, a_ref[bins, q * VW : (q + 1) * VW], NT)
-            fwd_send[...] = total.astype(BF16).reshape(NS, FPART, HALF)
-            to_slabs(phase, lambda w: fwd_send.at[w], fwd.at[k, s])
-            fwd[k, s] = fwd_send[s]
-            sent.append((phase, slabs_of(fwd.at[k])))
-            phase += 1
-        await_all(recv_sem.at[fwd_phase], slabs_of(fwd.at[k]))
-        summed = jnp.sum(fwd[k].astype(F32), axis=0)
-        ratio = (w_k * meas[:, bins]) / (w_k * summed + back[:, bins])
-        rat[k, s] = ratio.astype(BF16)
-        to_slabs(phase, lambda w: rat.at[k, s], rat.at[k, s])
-        rat_phase = phase
-        sent.append((rat_phase, slabs_of(rat.at[k])))
-        phase += 1
+            fwd_at = []
+            for h in range(STREAMS):
+                await_phase(img_at[h])
+                total = jnp.zeros((FS, HALF), F32)
+                for q in range(VQ):
+                    quarter = img[h, q * NS : (q + 1) * NS].astype(F32).reshape(FS, VW).astype(BF16)
+                    total = total + dot(quarter, a_ref[bins, q * VW : (q + 1) * VW], NT)
+                fwd_send[h] = total.reshape(NS, FPART, HALF).astype(BF16)
+                fwd_at.append(new_phase(slabs_of(fwd.at[k, h])))
+                to_slabs(fwd_at[h], lambda w: fwd_send.at[h, w], fwd.at[k, h, s])
+                fwd[k, h, s] = fwd_send[h, s]
+        for h in range(STREAMS):
+            await_phase(fwd_at[h])
+            summed = jnp.sum(fwd[k, h].astype(F32), axis=0)
+            ratio = (w_k * meas[h][:, bins]) / (w_k * summed + back[:, bins])
+            rat[k, h, s] = ratio.astype(BF16)
+            rat_at.append(new_phase(slabs_of(rat.at[k, h])))
+            to_slabs(rat_at[h], lambda w: rat.at[k, h, s], rat.at[k, h, s])
 
         if k == 0:
             row = lax.broadcasted_iota(jnp.int32, (16, BINS), 0)
@@ -253,69 +270,69 @@
             both = dot(lhs, a_ref[...], NN)
             for q in range(VQ):
                 sens_send[q] = both[0:SUBSETS, q * VW : (q + 1) * VW]
-            sens_phase = phase
-            phase += 1
-            to_views(sens_phase, lambda w: sens_send.at[lax.rem(w, VQ)], sens.at[v])
+            sens_at = new_phase(views_of(sens))
+            to_views(sens_at, lambda w: sens_send.at[lax.rem(w, VQ)], sens.at[v])
             sens[v] = sens_send[vi]
-            sent.append((sens_phase, views_of(sens)))
-
-        await_all(recv_sem.at[rat_phase], slabs_of(rat.at[k]))
-        lhs = rat[k].reshape(FR, HALF)
-        for q in range(VQ):
-            bck_send[k, q] = dot(lhs, a_ref[bins, q * VW : (q + 1) * VW], NN).astype(BF16)
-        to_views(
-            phase,
-            lambda w: bck_send.at[k, lax.rem(w, VQ), pl.ds(pl.multiple_of(part_of(w) * FPART, FPART), FPART), :],
-            bck.at[k, v],
+
+        for h in range(STREAMS):
+            await_phase(rat_at[h])
+            lhs = rat[k, h].astype(F32).reshape(FS, HALF).astype(BF16)
+            for q in range(VQ):
+                product = dot(lhs, a_ref[bins, q * VW : (q + 1) * VW], NN)
+                bck_send[k, h, q] = product.reshape(NS, FPART, VW).astype(BF16)
+            bck_at.append(new_phase(views_of(bck.at[k, h])))
+            to_views(bck_at[h], lambda w: bck_send.at[k, h, lax.rem(w, VQ), part_of(w)], bck.at[k, h, v])
+            bck[k, h, v] = bck_send[k, h, vi, fi]
+
+        if k == 0:
+            await_phase(sens_at)
+            sens_sum = jnp.sum(sens[...], axis=0)
+        img_at, halves = [], []
+        for h in range(STREAMS):
+            await_phase(bck_at[h])
+            back_image = jnp.sum(bck[k, h].astype(F32), axis=0)
+            est[h] = est[h] * (back_image + SMOOTH) / (sens_sum[k : k + 1, :] + SMOOTH)
+            halves.append(est[h].astype(BF16))
+            if k < SUBSETS - 1:
+                img_send[h] = halves[h]
+                img_at.append(new_phase(views_of(img.at[h])))
+                to_views(img_at[h], lambda w: img_send.at[h], img.at[h, slot])
+                img[h, slot] = halves[h]
+
+    part_sum = jnp.sum(halves[0].astype(F32), axis=0, keepdims=True)
+    for h in range(1, STREAMS):
+        part_sum = part_sum + jnp.sum(halves[h].astype(F32), axis=0, keepdims=True)
+    sum_send[...] = part_sum
+    sum_at = new_phase(views_of(sums))
+    to_views(sum_at, lambda w: sum_send, sums.at[v])
+    sums[v] = part_sum
+    partner = lax.rem(v + 16, NV)
+    pairs_at, pair_copies = [], []
+    for h in range(STREAMS):
+        fin[h, slot // 2, z] = est[h]
+        number = next(numbers)
+        pair_copies.append(
+            pltpu.make_async_remote_copy(
+                src_ref=fin.at[h, slot // 2, z], dst_ref=fin.at[h, slot // 2, z],
+                send_sem=send_sem.at[number], recv_sem=recv_sem.at[number],
+                device_id=(partner, s), device_id_type=MESH,
+            )
         )
-        bck[k, v] = bck_send[k, vi, frames, :]
-        bck_phase = phase
-        sent.append((bck_phase, views_of(bck.at[k])))
-        phase += 1
-
-        if k == 0:
-            await_all(recv_sem.at[sens_phase], views_of(sens))
-            sens_sum = jnp.sum(sens[...], axis=0)
-            est = est0
-        await_all(recv_sem.at[bck_phase], views_of(bck.at[k]))
-        back_image = jnp.sum(bck[k].astype(F32), axis=0)
-        est = est * (back_image + SMOOTH) / (sens_sum[k : k + 1, :] + SMOOTH)
-        half_image = est.astype(BF16)
-        if k < SUBSETS - 1:
-            img_send[...] = half_image
-            to_views(phase, lambda w: img_send, img.at[slot])
-            img[slot] = half_image
-            await_all(recv_sem.at[phase], views_of(img))
-            sent.append((phase, views_of(img)))
-            phase += 1
-
-    part_sum = jnp.sum(half_image.astype(F32), axis=0, keepdims=True)
-    sum_send[...] = part_sum
-    sum_phase = phase
-    to_views(sum_phase, lambda w: sum_send, sums.at[v])
-    sums[v] = part_sum
-    pair_phase, fin_phase = phase + 1, phase + 2
-    phase += 3
-    partner = lax.rem(v + 16, NV)
-    fin[slot // 2, z] = est
-    pair_copy = pltpu.make_async_remote_copy(
-        src_ref=fin.at[slot // 2, z], dst_ref=fin.at[slot // 2, z],
-        send_sem=send_sem.at[pair_phase], recv_sem=recv_sem.at[pair_phase],
-        device_id=(partner, s), device_id_type=MESH,
-    )
-    pair_copy.start()
-    await_all(recv_sem.at[sum_phase], views_of(sums))
-    sent.append((sum_phase, views_of(sums)))
-    pair_copy.wait_recv()
-
-    @pl.loop(1, 16)
-    def _(i):
-        w = 16 * z + lax.rem(lax.rem(v, 16) + i, 16)
-        pltpu.make_async_remote_copy(
-            src_ref=fin.at[slot // 2], dst_ref=fin.at[slot // 2],
-            send_sem=send_sem.at[fin_phase], recv_sem=recv_sem.at[fin_phase],
-            device_id=(w, s), device_id_type=MESH,
-        ).start()
+        pair_copies[h].start()
+    await_phase(sum_at)
+    fin_at = []
+    for h in range(STREAMS):
+        pair_copies[h].wait_recv()
+        fin_at.append(new_phase(fin.at[h, pl.ds(0, 15)]))
+
+        @pl.loop(1, 16)
+        def _(i):
+            w = 16 * z + lax.rem(lax.rem(v, 16) + i, 16)
+            pltpu.make_async_remote_copy(
+                src_ref=fin.at[h, slot // 2], dst_ref=fin.at[h, slot // 2],
+                send_sem=send_sem.at[fin_at[h]], recv_sem=recv_sem.at[fin_at[h]],
+                device_id=(w, s), device_id_type=MESH,
+            ).start()
 
     quarter = []
     for q in range(VQ):
@@ -329,36 +346,35 @@
     lhs = jnp.where(row == 0, hi, jnp.where(row == 1, mid, jnp.where(row == 2, low, 0.0))).astype(BF16)
     bins_sum = jnp.sum(dot(lhs, a_ref[...], NT), axis=0, keepdims=True)
     q_send[...] = bins_sum
-    to_slabs(phase, lambda w: q_send, q_recv.at[s])
+    q_at = new_phase(slabs_of(q_recv))
+    to_slabs(q_at, lambda w: q_send, q_recv.at[s])
     q_recv[s] = bins_sum
-    await_all(recv_sem.at[phase], slabs_of(q_recv))
-    sent.append((phase, slabs_of(q_recv)))
-    phase += 1
+    await_phase(q_at)
     final = jnp.sum(q_recv[...], axis=0)
     expected = weight * final + FR * back
     fan_exp = fan(jnp.concatenate([expected, expected], axis=1), oh_hi, oh_lo)
     fan_send[:, 1:2, :] = fan_exp.reshape(NV, 1, TB)
-    to_views(phase, lambda w: fan_send.at[w], fan_recv.at[v])
+    fan_at = new_phase(views_of(fan_recv))
+    to_views(fan_at, lambda w: fan_send.at[w], fan_recv.at[v])
     fan_recv[v] = fan_send[v]
 
-    others = fin.at[pl.ds(0, 15)]
-    await_all(recv_sem.at[fin_phase], others)
+    for h in range(STREAMS):
+        await_phase(fin_at[h])
     for q in range(VQ):
-        part = pl.ds(q * VW, VW)
-        out_ref[part, :] = fin[q * 4 : (q + 1) * 4].reshape(FR, VW).T
-
-    await_all(recv_sem.at[phase], views_of(fan_recv))
+        block = fin[:, q * 4 : (q + 1) * 4].reshape(FR, VW)
+        out_ref[pl.ds(q * VW, VW), :] = block.T
+
+    await_phase(fan_at)
     totals = jnp.sum(fan_recv[...], axis=0)
     gain = eff_ref[0] * (totals[0:1, :] + FAN_OFFSET) / (totals[1:2, :] + FAN_OFFSET)
     gain_ref[...] = gain[:, 0:OWN]
-    sent.append((phase, views_of(fan_recv)))
-    sent.append((fin_phase, others))
     for number, ref in sent:
         await_all(send_sem.at[number], ref)
-    pair_copy.wait_send()
-
-
-PHASES = 14
+    for copy in pair_copies:
+        copy.wait_send()
+
+
+PHASES = 5 + STREAMS * (4 * SUBSETS + 1)
 
 
 def on_device(
@@ -388,21 +404,21 @@
             VMEM((NB, TB, FR), F32),
             VMEM((FR, VOX), F32),
             VMEM((FR, BINS), F32),
-            VMEM((NS, FPART, HALF), BF16),
+            VMEM((STREAMS, NS, FPART, HALF), BF16),
             VMEM((1, 1, TB), F32),
             VMEM((NV, 1, TB), F32),
-            VMEM((NS, FPART, HALF), BF16),
-            VMEM((SUBSETS, NS, FPART, HALF), BF16),
-            VMEM((SUBSETS, NS, FPART, HALF), BF16),
+            VMEM((STREAMS, NS, FPART, HALF), BF16),
+            VMEM((SUBSETS, STREAMS, NS, FPART, HALF), BF16),
+            VMEM((SUBSETS, STREAMS, NS, FPART, HALF), BF16),
             VMEM((VQ, SUBSETS, VW), F32),
             VMEM((NV, SUBSETS, VW), F32),
-            VMEM((SUBSETS, VQ, FR, VW), BF16),
-            VMEM((SUBSETS, NV, FPART, VW), BF16),
-            VMEM((FPART, VW), BF16),
-            VMEM((NV, FPART, VW), BF16),
+            VMEM((SUBSETS, STREAMS, VQ, NS, FPART, VW), BF16),
+            VMEM((SUBSETS, STREAMS, NV, FPART, VW), BF16),
+            VMEM((STREAMS, FPART, VW), BF16),
+            VMEM((STREAMS, NV, FPART, VW), BF16),
             VMEM((1, VW), F32),
             VMEM((NV, 1, VW), F32),
-            VMEM((NV // 2, 2, FPART, VW), F32),
+            VMEM((STREAMS, NV // 2, 2, FPART, VW), F32),
             VMEM((1, BINS), F32),
             VMEM((NS, 1, BINS), F32),
             VMEM((NV, 2, TB), F32),

time: 76.1 us -> 72.8 us (0.957)
  Pallas kernels: 73.3 us -> 70 us
    pallas_call x1, Pallas kernels: 73.3 us -> 70 us  [on_device(): pl.pallas_call(exchange, out_shape=(VMEM((VOX, FR), F32), VMEM((1, OWN),...]
where the time goes in v4:
time: 72.8 us; the launch traced here: 72.6 us
  Pallas kernels  70 us (96%)
  local copies, waits for them, and re-layouts  1.31 us (2%)
  between operations  1.29 us (2%)
    pallas_call x1, Pallas kernels, on_device(): pl.pallas_call(exchange, out_shape=(VMEM((VOX, FR), F32), VMEM((1, OWN),...  70 us

profile of v4, /device:TPU:1, one launch (start us, length us, event | category | flops | bytes accessed | tf_op | source)
XLA Modules:
  0.0 72.6 jit_solution(2591006062714556727)
XLA Ops:
  1.3 70.0 %exchange.1 = (f32[1024,128]{1,0:T(8,128)S(1)}, f32[1,105]{1,0:T(1,128)S(1)}) custom-call(s32[1,1]{1,0:T(1,128)S(6)} %copy.16.tile_count, s32[8]{0:T(128)} %subset.1, s32[1,64]{1,0:T(1,128)} %bitcast.13, s32[1,64]{1,0:T(1,128)} %bitcast.14, s32[2,1024]{1,0:T(2,128)} %pairs.1, f32[1,1024]{1,0:T(1,128)} %bitcast.12, f32[1,105]{1,0:T(1,128)} %bitcast.15, ...), custom_call_target="tpu_custom_call" | custom-call | tf_op jit(solution)/shard_map/exchange/pallas_call | solution.py:389
  71.3 0.8 %copy.14 = f32[1024,128]{1,0:T(8,128)} copy(f32[1024,128]{1,0:T(8,128)S(1)} %get-tuple-element.6) | data formatting | bytes 1048576
  72.1 0.5 copy.15
